TPU v7x, 32 devices: a whole 2x2x4 slice. The times are simulated.
32 devices in a mesh: nodes: 8 (over z, x), feat: 4 (over y, core).
Axes of the slice: x: 2, y: 2, z: 4, core: 2. Of those that a mesh axis runs over, the one named last changes fastest.
Arguments:
- features: bfloat16 [128, 32768], P('feat', 'nodes'), may hold values from -6 to 6
- w_self: bfloat16 [128, 256], replicated, may hold values from -0.5 to 0.5
- w_neigh: bfloat16 [128, 256], replicated, may hold values from -0.5 to 0.5
- hidden_bias: float32 [256], replicated, may hold values from -3 to 3
- cotangent: bfloat16 [256, 32768], P('feat', 'nodes'), may hold values from -0.032958984 to 0.032958984
- hub_local: int32 [8, 32], P('nodes'), may hold values from 0 to 4095
- send_rows: int32 [8, 8, 128], P('nodes'), may hold values from 0 to 4095
- send_count: int32 [8, 8], P('nodes'), may hold values from 0 to 128, as said below
- tile_values: bfloat16 [1024, 128, 128], P('nodes'), may hold values from 0 to 0.039794922
- tile_target: int32 [8, 128], P('nodes'), may hold values from 0 to 31, as said below
- tile_anchor: int32 [8, 128], P('nodes'), may hold values from 0 to 41, as said below
- tile_count: int32 [8], P('nodes'), may hold values from 42 to 128, as said below
Outputs:
- hidden: bfloat16 [256, 32768], P('feat', 'nodes')
- grad_self: float32 [128, 256], P(None, 'feat')
- grad_neigh: float32 [128, 256], P(None, 'feat')
- bias_grad: float32 [256], P('feat')
Inputs may be any that keep to these rules, and one draw needn't show every extreme that they name: hub_local[q, j] is the local row of partition q's j-th hub node; hubs are ordered by owner, then by j. send_rows[q, p, j] is the local row of partition q that fills slot j of what q sends to p; slots at or after send_count[q, p] are padding. `send_count`: A partition sends nothing to itself, and every partition fills all 128 slots for at least one other partition. `tile_target`: A block is 128 consecutive local nodes. On every partition each block is the destination of some live tile. `tile_anchor`: A block is 128 consecutive rows of source_p. On every partition each source block that holds halo or hub rows is used by some live tile. Tile slots at or after tile_count[p] are padding: their tile_values, tile_target and tile_anchor entries are arbitrary and must be ignored. Some partition fills all 128 slots.
All inputs are finite; a program needn't handle non-finite values.
Results may differ from a plain program's by a relative error of at most 0.0055.
Values may be sent and summed in bfloat16 or wider, within the bound.
No kernel may reach another device: no remote copies, remote signals or barrier semaphores. Data moves between devices by JAX's collectives and lax.ppermute only.
A program may use at most 64 MiB of HBM per device.

v0:
```python
import jax
import jax.numpy as jnp
from jax import lax
from jax.sharding import PartitionSpec as P

TSTEP = 32


def local(
    features,
    w_self,
    w_neigh,
    hidden_bias,
    cotangent,
    hub_local,
    send_rows,
    send_count,
    tile_values,
    tile_target,
    tile_anchor,
    tile_count,
):
    node_parts = lax.axis_size("nodes")
    feat_parts = lax.axis_size("feat")
    feat_index = lax.axis_index("feat")
    width_local, node_local = features.shape
    slot_count = send_rows.shape[2]
    hub_count = hub_local.shape[1]
    tile_size = tile_values.shape[1]
    hidden_local = w_self.shape[1] // feat_parts
    own_hubs = jnp.take(features, hub_local[0], axis=1)
    outgoing = jnp.take(features, send_rows[0].reshape(-1), axis=1).reshape(
        width_local, node_parts, slot_count
    )
    live_slot = (
        lax.broadcasted_iota(jnp.int32, (node_parts, slot_count), 1) < send_count[0][:, None]
    )
    outgoing = jnp.where(live_slot[None], outgoing, jnp.zeros_like(outgoing))
    copies = jnp.broadcast_to(own_hubs[:, None, :], (width_local, node_parts, hub_count))
    halo_rows, hub_parts = (
        lax.all_to_all(outgoing, "nodes", split_axis=1, concat_axis=1, tiled=True),
        lax.all_to_all(copies, "nodes", split_axis=1, concat_axis=1, tiled=True),
    )
    hub_rows = hub_parts.reshape(width_local, node_parts * hub_count)
    source_rows = jnp.concatenate(
        [features, halo_rows.reshape(width_local, node_parts * slot_count), hub_rows], axis=1
    )
    source_blocks = source_rows.reshape(width_local, -1, tile_size)
    local_blocks = node_local // tile_size
    live_count = tile_count[0]
    turns = (live_count + TSTEP - 1) // TSTEP
    block_ids = jnp.arange(local_blocks, dtype=jnp.int32)

    def one_turn(turn_index, running):
        first_tile = turn_index * TSTEP
        tile_block = lax.dynamic_slice_in_dim(tile_values, first_tile, TSTEP, 0)
        targets = lax.dynamic_slice_in_dim(tile_target[0], first_tile, TSTEP, 0)
        anchors = lax.dynamic_slice_in_dim(tile_anchor[0], first_tile, TSTEP, 0)
        live_tiles = first_tile + jnp.arange(TSTEP, dtype=jnp.int32) < live_count
        picked = jnp.take(source_blocks, anchors, axis=1)
        products = jnp.einsum(
            "ftk,tik->fti", picked, tile_block, preferred_element_type=jnp.float32
        )
        selector = ((targets[:, None] == block_ids[None, :]) & live_tiles[:, None]).astype(
            jnp.float32
        )
        return running + jnp.einsum(
            "fti,tn->fni", products, selector, precision=lax.Precision.HIGHEST
        )

    empty = jnp.zeros((width_local, local_blocks, tile_size), jnp.float32)
    aggregate = (
        lax.fori_loop(0, turns, one_turn, empty)
        .reshape(width_local, node_local)
        .astype(jnp.bfloat16)
    )
    contract_first = (((0,), (0,)), ((), ()))
    contract_last = (((1,), (1,)), ((), ()))
    full_inputs, full_aggregate = (
        lax.all_gather(features, "feat", axis=0, tiled=True),
        lax.all_gather(aggregate, "feat", axis=0, tiled=True),
    )
    self_cols = lax.dynamic_slice_in_dim(w_self, feat_index * hidden_local, hidden_local, 1)
    neigh_cols = lax.dynamic_slice_in_dim(w_neigh, feat_index * hidden_local, hidden_local, 1)
    preact = lax.dot_general(
        self_cols, full_inputs, contract_first, preferred_element_type=jnp.float32
    )
    preact = preact + lax.dot_general(
        neigh_cols, full_aggregate, contract_first, preferred_element_type=jnp.float32
    )
    bias_local = lax.dynamic_slice_in_dim(hidden_bias, feat_index * hidden_local, hidden_local, 0)
    preact = preact + bias_local[:, None]
    sigmoid_value = jax.nn.sigmoid(preact)
    hidden = (preact * sigmoid_value).astype(jnp.bfloat16)
    pre_grad = (
        cotangent.astype(jnp.float32) * sigmoid_value * (1.0 + preact * (1.0 - sigmoid_value))
    ).astype(jnp.bfloat16)
    bias_part = jnp.sum(pre_grad, axis=1, dtype=jnp.float32)
    own_grad = lax.dot_general(
        full_inputs, pre_grad, contract_last, preferred_element_type=jnp.float32
    )
    neigh_grad = lax.dot_general(
        full_aggregate, pre_grad, contract_last, preferred_element_type=jnp.float32
    )
    weight_part = jnp.stack([own_grad, neigh_grad])
    weight_total, bias_grad = lax.psum((weight_part, bias_part), "nodes")
    return (hidden, weight_total[0], weight_total[1], bias_grad)


def solution(mesh):
    in_specs = (
        P("feat", "nodes"),
        P(),
        P(),
        P(),
        P("feat", "nodes"),
        P("nodes", None),
        P("nodes", None, None),
        P("nodes", None),
        P("nodes", None, None),
        P("nodes", None),
        P("nodes", None),
        P("nodes"),
    )
    out_specs = (P("feat", "nodes"), P(None, "feat"), P(None, "feat"), P("feat"))
    return jax.shard_map(local, mesh=mesh, in_specs=in_specs, out_specs=out_specs, check_vma=False)
```

profile of v0, /device:TPU:0, one launch (start us, length us, event | category | flops | bytes accessed | tf_op | source)
XLA Modules:
  0.0 152.6 jit_solution(10035392069236234365)
XLA Ops:
  7.2 0.0 copy-start
  7.2 0.0 copy-start.4
  7.2 0.0 copy-start.7
  7.2 0.7 fusion.22
  7.9 0.7 compare_and_fusion.2
  8.6 1.4 copy.32
  10.0 0.6 gather_fusion.2
  10.6 0.1 select_bitcast_fusion
  10.7 0.1 copy.36
  10.8 0.7 reshape.199
  11.5 7.3 %all-to-all-start.1 = ((bf16[8,2,512]{2,1,0:T(2,128)(2,1)}), bf16[8,2,512]{2,1,0:T(2,128)(2,1)S(1)}, u32[]{:S(2)}, u32[]{:S(2)}) async-start(bf16[8,2,512]{2,1,0:T(2,128)(2,1)} %reshape.199), calls=%async_computation.1 | async-start | bytes 32768 | tf_op jit(solution)/shard_map/all_to_all | solution.py:42
  18.8 0.8 iota_compare_fusion.1
  19.6 0.7 compare_select_fusion.2
  20.3 3.2 %gather_fusion.1 = bf16[1024,32]{1,0:T(8,128)(2,1)S(1)} fusion(bf16[32,4096]{0,1:T(8,128)(2,1)S(1)} %copy.32, s32[1024]{0:T(1024)S(1)} %broadcast_clamp_fusion), kind=kCustom, calls=%fused_computation.1 | custom fusion | bytes 135168 | tf_op jit(solution)/shard_map/jit(_take)/gather | solution.py:32
  23.5 0.1 copy.33
  23.6 0.6 select_select_fusion
  24.3 1.1 all-to-all-done.1
  25.4 4.9 %all-to-all-start = ((bf16[32,8,128]{2,0,1:T(8,128)(2,1)}), bf16[32,8,128]{2,0,1:T(8,128)(2,1)S(1)}, u32[]{:S(2)}, u32[]{:S(2)}) async-start(bf16[32,8,128]{2,0,1:T(8,128)(2,1)} %select_select_fusion), calls=%async_computation | async-start | bytes 131072 | tf_op jit(solution)/shard_map/all_to_all | solution.py:41
  30.3 0.0 all-gather.3.cloned.1.call-start
  30.3 0.7 all-gather.3.cloned.1.call-update
  31.0 0.0 all-gather.5.cloned.1.call-start
  31.7 0.1 reshape.200
  31.8 0.1 reshape.169
  32.0 5.2 %all-to-all-done = bf16[32,8,128]{2,0,1:T(8,128)(2,1)S(1)} async-done(((bf16[32,8,128]{2,0,1:T(8,128)(2,1)}), bf16[32,8,128]{2,0,1:T(8,128)(2,1)S(1)}, u32[]{:S(2)}, u32[]{:S(2)}) %all-to-all-start) | async-done | bytes 65568 | tf_op jit(solution)/shard_map/all_to_all | solution.py:41
  37.2 1.0 copy_bitcast_fusion
  38.2 0.1 broadcast_in_dim.55
  38.2 0.0 copy-done.4
  38.2 0.0 copy-done.7
  38.3 0.0 copy-start.6
  38.3 0.0 copy-start.3
  38.3 0.0 copy-start.5
  38.3 8.6 %while.11 = (s32[]{:T(128)}, f32[32,32,128]{2,1,0:T(8,128)S(1)}, s32[]{:T(128)}, s32[1,128]{1,0:T(1,128)S(1)}, s32[]{:T(128)}, /*index=5*/bf16[128,128,128]{2,1,...) while((s32[]{:T(128)}, f32[32,32,128]{2,1,0:T(8,128)S(1)}, ...), condition=%wide.region_1.2_spmd.clone, body=%wide.region_0.1_spmd.clone.sunk | while | flops 84151648 | bytes 3937595 | solution.py:73
  38.3 0.1 fusion.44
  38.4 0.1 fusion.43
  38.5 0.7 compare_and_fusion.4
  39.2 0.6 gather_fusion
  39.8 2.0 %convolution_bitcast_fusion.5 = f32[32,32,128]{2,0,1:T(8,128)S(1)} fusion(bf16[128,128,128]{2,1,0:T(8,128)(2,1)} %get-tuple-element.204, s32[]{:T(128)S(6)} %select_n.130, bf16[32,32,128]{2,1,0:T(8,128)(2,1)S(1)} %gather_fusion, pred[32]{0:T(512)(128)(4,1)S(1)} %get-tuple-element.173), kind=kOutput, calls=%fused_computation.5.clone.1 | convolution fusion | flops 33685504 | bytes 1835044 | tf_op jit(solution)/shard_map/while/body/ftk,tik->fti/dot_general | solution.py:61
  41.8 0.8 fusion.45
  42.6 0.1 fusion.44
  42.7 0.1 fusion.43
  42.8 0.7 compare_and_fusion.4
  43.5 0.6 gather_fusion
  44.1 1.9 %convolution_bitcast_fusion.5 = f32[32,32,128]{2,0,1:T(8,128)S(1)} fusion(bf16[128,128,128]{2,1,0:T(8,128)(2,1)} %get-tuple-element.204, s32[]{:T(128)S(6)} %select_n.130, bf16[32,32,128]{2,1,0:T(8,128)(2,1)S(1)} %gather_fusion, pred[32]{0:T(512)(128)(4,1)S(1)} %get-tuple-element.173), kind=kOutput, calls=%fused_computation.5.clone.1 | convolution fusion | flops 33685504 | bytes 1835044 | tf_op jit(solution)/shard_map/while/body/ftk,tik->fti/dot_general | solution.py:61
  46.0 0.8 fusion.45
  46.9 0.8 copy.47
  47.7 0.0 all-gather.5.cloned.1.call-update
  47.7 0.0 all-reduce.2.cloned.1.call-start
  47.8 0.0 copy-done.6
  47.8 0.1 dynamic_slice.24
  47.9 2.9 %all-gather.3.cloned.1.call-done = bf16[128,4096]{1,0:T(8,128)(2,1)} async-done(((bf16[32,4096]{1,0:T(8,128)(2,1)}), bf16[128,4096]{1,0:T(8,128)(2,1)}) %all-gather.3.cloned.1.call-update) | async-done | bytes 1048592 | tf_op jit(solution)/shard_map/all_gather | solution.py:80
  50.8 0.0 copy-done.3
  50.8 1.6 %fusion.20 = f32[64,4096]{1,0:T(8,128)S(1)} fusion(bf16[128,4096]{1,0:T(8,128)(2,1)} %all-gather.3.cloned.1.call-done, bf16[128,256]{1,0:T(8,128)(2,1)S(1)} %copy-done.3, s32[]{:T(128)S(6)} %select_n.85), kind=kOutput, calls=%fused_computation.46 | convolution fusion | flops 67108864 | bytes 2129924 | tf_op jit(solution)/shard_map/dot_general | solution.py:85
  52.4 0.0 copy-start.1
  52.4 18.1 %all-gather.5.cloned.1.call-done = bf16[128,4096]{1,0:T(8,128)(2,1)} async-done(((bf16[32,4096]{1,0:T(8,128)(2,1)}), bf16[128,4096]{1,0:T(8,128)(2,1)}) %all-gather.5.cloned.1.call-update) | async-done | bytes 1048592 | tf_op jit(solution)/shard_map/all_gather | solution.py:81
  70.5 0.0 copy-done
  70.5 0.0 copy-done.5
  70.5 3.0 %convert_reduce_fusion = (f32[64]{0:T(128)S(1)}, bf16[64,4096]{1,0:T(8,128)(2,1)S(1)}, bf16[64,4096]{1,0:T(8,128)(2,1)}) fusion(bf16[64,4096]{1,0:T(8,128)(2,1)S(1)} %copy-done.5, f32[64]{0:T(128)S(1)} %dynamic_slice.24, f32[64,4096]{1,0:T(8,128)S(1)} %fusion.20, bf16[128,4096]{1,0:T(8,128)(2,1)} %all-gather.5.cloned.1.call-done, ...), kind=kOutput, calls=%fused_computation.33 | convolution fusion | flops 71303104 | bytes 3703556 | tf_op jit(solution)/shard_map/dot_general | solution.py:88
  73.5 0.5 convolution_bitcast_fusion.2
  74.0 0.5 convolution_bitcast_fusion.3
  74.5 0.6 pad_maximum_fusion
  75.2 0.0 all-reduce.2.cloned.1.call-update
  75.2 21.9 %psum.15 = f32[64]{0:T(128)} all-reduce(f32[64]{0:T(128)S(1)} %get-tuple-element.112), channel_id=1, replica_groups=mesh['nodes'=8,'feat'=4] {'nodes'}, use_global_device_ids=true, to_apply=%region_4.5 | all-reduce | flops 64 | bytes 512 | tf_op jit(solution)/shard_map/psum | solution.py:106
  97.0 47.6 %all-reduce.2.cloned.1.call-done = f32[2,128,64]{1,2,0:T(8,128)} async-done(((f32[2,128,64]{1,2,0:T(8,128)}), f32[2,128,64]{1,2,0:T(8,128)}) %all-reduce.2.cloned.1.call-update) | async-done | bytes 65552 | tf_op jit(solution)/shard_map/psum | solution.py:106
  144.6 1.4 slice_bitcast_fusion
  (11 shorter events, 0.1 us)
Async XLA Ops:
  7.2 63.4 %copy-start = (bf16[128,256]{1,0:T(8,128)(2,1)S(1)}, bf16[128,256]{1,0:T(8,128)(2,1)}, u32[]{:S(2)}) copy-start(bf16[128,256]{1,0:T(8,128)(2,1)} %param.16) | copy-start | bytes 196612
  7.2 31.1 %copy-start.4 = (s32[1,128]{1,0:T(1,128)S(1)}, s32[1,128]{1,0:T(1,128)}, u32[]{:S(2)}) copy-start(s32[1,128]{1,0:T(1,128)} %param.24) | copy-start | bytes 1540
  7.2 31.1 %copy-start.7 = (s32[1,128]{1,0:T(1,128)S(1)}, s32[1,128]{1,0:T(1,128)}, u32[]{:S(2)}) copy-start(s32[1,128]{1,0:T(1,128)} %param.23) | copy-start | bytes 1540
  11.5 13.9 %all-to-all-start.1 = ((bf16[8,2,512]{2,1,0:T(2,128)(2,1)}), bf16[8,2,512]{2,1,0:T(2,128)(2,1)S(1)}, u32[]{:S(2)}, u32[]{:S(2)}) async-start(bf16[8,2,512]{2,1,0:T(2,128)(2,1)} %reshape.199), calls=%async_computation.1 | async-start | bytes 32768 | tf_op jit(solution)/shard_map/all_to_all | solution.py:42
  25.4 11.8 %all-to-all-start = ((bf16[32,8,128]{2,0,1:T(8,128)(2,1)}), bf16[32,8,128]{2,0,1:T(8,128)(2,1)S(1)}, u32[]{:S(2)}, u32[]{:S(2)}) async-start(bf16[32,8,128]{2,0,1:T(8,128)(2,1)} %select_select_fusion), calls=%async_computation | async-start | bytes 131072 | tf_op jit(solution)/shard_map/all_to_all | solution.py:41
  30.3 20.5 %all-gather.3.cloned.1.call-start = ((), (), s32[]{:S(2)}) async-start(), calls=%async_computation.2 | async-start | bytes 1310720 | tf_op jit(solution)/shard_map/all_gather | solution.py:80
  31.0 39.5 %all-gather.5.cloned.1.call-start = ((), (), s32[]{:S(2)}) async-start(), calls=%async_computation.3 | async-start | bytes 1310720 | tf_op jit(solution)/shard_map/all_gather | solution.py:81
  38.3 9.5 %copy-start.6 = (f32[256]{0:T(256)S(1)}, f32[256]{0:T(256)}, u32[]{:S(2)}) copy-start(f32[256]{0:T(256)} %param.17) | copy-start | bytes 3076
  38.3 12.5 %copy-start.3 = (bf16[128,256]{1,0:T(8,128)(2,1)S(1)}, bf16[128,256]{1,0:T(8,128)(2,1)}, u32[]{:S(2)}) copy-start(bf16[128,256]{1,0:T(8,128)(2,1)} %param.15) | copy-start | bytes 196612
  38.3 32.2 %copy-start.5 = (bf16[64,4096]{1,0:T(8,128)(2,1)S(1)}, bf16[64,4096]{1,0:T(8,128)(2,1)}, u32[]{:S(2)}) copy-start(bf16[64,4096]{1,0:T(8,128)(2,1)} %param.18) | copy-start | bytes 1572868
  47.7 96.9 %all-reduce.2.cloned.1.call-start = ((), (), s32[]{:S(2)}) async-start(), calls=%async_computation.4 | async-start | bytes 131072 | tf_op jit(solution)/shard_map/psum | solution.py:106
  52.4 21.6 %copy-start.1 = (bf16[128,4096]{1,0:T(8,128)(2,1)S(1)}, bf16[128,4096]{1,0:T(8,128)(2,1)}, u32[]{:S(2)}) copy-start(bf16[128,4096]{1,0:T(8,128)(2,1)} %all-gather.3.cloned.1.call-done) | copy-start | bytes 3145732
  70.5 3.0 %copy-start.2 = (bf16[128,4096]{1,0:T(8,128)(2,1)S(1)}, bf16[128,4096]{1,0:T(8,128)(2,1)}, u32[]{:S(2)}) copy-start(bf16[128,4096]{1,0:T(8,128)(2,1)} %all-gather.5.cloned.1.call-done) | copy-start | bytes 3145732
Sparse Core Ops, SparseCore 0:
  32.6 18.1 all-gather.2
  52.9 17.5 all-gather.4
  75.3 69.2 all-reduce.1
where the time goes:
time: 153 us
  waiting for transfers between devices  75.6 us (49%)
  blocking collectives  21.9 us (14%)
  between operations  14.6 us (10%)
  starting transfers between devices  12.3 us (8%)
  matrix products  11.1 us (7%)
  local copies, waits for them, and re-layouts  10.2 us (7%)
  other arithmetic  6.84 us (4%)
    psum x1, waiting for transfers between devices, local(): weight_total, bias_grad = lax.psum((weight_part, bias_part), 'nodes')  47.6 us
    psum x1, blocking collectives, local(): weight_total, bias_grad = lax.psum((weight_part, bias_part), 'nodes')  21.9 us
    all_gather x1, waiting for transfers between devices, local(): lax.all_gather(aggregate, 'feat', axis=0, tiled=True)  18.1 us
    all_to_all x1, starting transfers between devices, local(): lax.all_to_all(copies, 'nodes', split_axis=1, concat_axis=1, tiled=True)  7.28 us
    all_to_all x1, waiting for transfers between devices, local(): lax.all_to_all(outgoing, 'nodes', split_axis=1, concat_axis=1, tiled=True)  5.21 us
    all_to_all x1, starting transfers between devices, local(): lax.all_to_all(outgoing, 'nodes', split_axis=1, concat_axis=1, tiled=True)  4.89 us
    dot_general x2, matrix products, one_turn(): jnp.einsum('ftk,tik->fti', picked, tile_block, preferred_element_type=jnp...  3.87 us
    gather x2, local copies, waits for them, and re-layouts, local(): jnp.take(features, send_rows[0].reshape(-1), axis=1)  3.33 us
  transfers between devices with their start and end apart: 5, of which 5 were waited for; matrix products, arithmetic and copies ran while one was open for 12% of the time, Pallas kernels for 0%

commit v1 on v0

--- a/solution.py
+++ b/solution.py
@@ -4,6 +4,29 @@
 from jax.sharding import PartitionSpec as P
 
 TSTEP = 32
+
+
+def laid_out(blocks, dim):
+    shape = list(blocks.shape[1:])
+    shape[dim] *= blocks.shape[0]
+    return jnp.moveaxis(blocks, 0, dim).reshape(shape)
+
+
+def grow_blocks(array, axis):
+    count, index = (lax.axis_size(axis), lax.axis_index(axis))
+    tiles, distance = (array[None], 1)
+    while distance < count:
+        partner_block = lax.ppermute(tiles, axis, [(i, i ^ distance) for i in range(count)])
+        low = index & distance == 0
+        tiles = jnp.concatenate(
+            [jnp.where(low, tiles, partner_block), jnp.where(low, partner_block, tiles)]
+        )
+        distance *= 2
+    return tiles
+
+
+def doubled_up(x, axis, dim):
+    return laid_out(grow_blocks(x, axis), dim)
 
 
 def local(
@@ -78,7 +101,7 @@
     contract_last = (((1,), (1,)), ((), ()))
     full_inputs, full_aggregate = (
         lax.all_gather(features, "feat", axis=0, tiled=True),
-        lax.all_gather(aggregate, "feat", axis=0, tiled=True),
+        doubled_up(aggregate, "feat", 0),
     )
     self_cols = lax.dynamic_slice_in_dim(w_self, feat_index * hidden_local, hidden_local, 1)
     neigh_cols = lax.dynamic_slice_in_dim(w_neigh, feat_index * hidden_local, hidden_local, 1)

time: 153 us -> 159 us (1.039)
  waiting for transfers between devices: 75.6 us -> 78.9 us
  blocking collectives: 21.9 us -> 24.2 us
  starting transfers between devices: 12.3 us -> 13.9 us
    all_gather x1 -> x0, waiting for transfers between devices: 18.1 us -> none  [local(): lax.all_gather(aggregate, 'feat', axis=0, tiled=True)]
    ppermute x0 -> x2, waiting for transfers between devices: none -> 13.8 us  [grow_blocks(): lax.ppermute(tiles, axis, [(i, i ^ distance) for i in range(count)])]
    all_gather x1, waiting for transfers between devices: 2.9 us -> 9.2 us  [local(): lax.all_gather(features, 'feat', axis=0, tiled=True)]
    psum x1, blocking collectives: 21.9 us -> 24.2 us  [local(): weight_total, bias_grad = lax.psum((weight_part, bias_part), 'nodes')]
    ppermute x0 -> x2, starting transfers between devices: none -> 1.65 us  [grow_blocks(): lax.ppermute(tiles, axis, [(i, i ^ distance) for i in range(count)])]
  transfers between devices with their start and end apart: 5 -> 6, of which waited for: 5 -> 6; matrix products, arithmetic and copies ran while one was open for 12% -> 4% of each run, Pallas kernels for 0% -> 0%
where the time goes in v1:
time: 159 us; the launch traced here: 158 us
  waiting for transfers between devices  78.9 us (50%)
  blocking collectives  24.2 us (15%)
  between operations  15 us (9%)
  starting transfers between devices  13.9 us (9%)
  matrix products  9.78 us (6%)
  local copies, waits for them, and re-layouts  9.46 us (6%)
  other arithmetic  7.09 us (4%)
    psum x1, waiting for transfers between devices, local(): weight_total, bias_grad = lax.psum((weight_part, bias_part), 'nodes')  48.8 us
    psum x1, blocking collectives, local(): weight_total, bias_grad = lax.psum((weight_part, bias_part), 'nodes')  24.2 us
    ppermute x2, waiting for transfers between devices, grow_blocks(): lax.ppermute(tiles, axis, [(i, i ^ distance) for i in range(count)])  13.8 us
    all_gather x1, waiting for transfers between devices, local(): lax.all_gather(features, 'feat', axis=0, tiled=True)  9.2 us
    all_to_all x1, starting transfers between devices, local(): lax.all_to_all(copies, 'nodes', split_axis=1, concat_axis=1, tiled=True)  7.28 us
    all_to_all x1, waiting for transfers between devices, local(): lax.all_to_all(outgoing, 'nodes', split_axis=1, concat_axis=1, tiled=True)  5.94 us
    all_to_all x1, starting transfers between devices, local(): lax.all_to_all(outgoing, 'nodes', split_axis=1, concat_axis=1, tiled=True)  4.89 us
    dot_general x2, matrix products, one_turn(): jnp.einsum('ftk,tik->fti', picked, tile_block, preferred_element_type=jnp...  3.83 us
  transfers between devices with their start and end apart: 6, of which 6 were waited for; matrix products, arithmetic and copies ran while one was open for 4% of the time, Pallas kernels for 0%

profile of v1, /device:TPU:0, one launch (start us, length us, event | category | flops | bytes accessed | tf_op | source)
XLA Modules:
  0.0 158.3 jit_solution(18238799915872073263)
XLA Ops:
  7.2 0.0 copy-start
  7.2 0.0 copy-start.3
  7.2 0.0 copy-start.6
  7.2 0.7 fusion.22
  7.9 0.7 compare_and_fusion.2
  8.6 1.4 copy.32
  10.0 0.6 gather_fusion.2
  10.6 0.1 select_bitcast_fusion
  10.7 0.1 copy.36
  10.8 0.7 reshape.213
  11.5 7.3 %all-to-all-start.1 = ((bf16[8,2,512]{2,1,0:T(2,128)(2,1)}), bf16[8,2,512]{2,1,0:T(2,128)(2,1)S(1)}, u32[]{:S(2)}, u32[]{:S(2)}) async-start(bf16[8,2,512]{2,1,0:T(2,128)(2,1)} %reshape.213), calls=%async_computation.1 | async-start | bytes 32768 | tf_op jit(solution)/shard_map/all_to_all | solution.py:65
  18.8 0.8 iota_compare_fusion.1
  19.6 0.7 compare_select_fusion.2
  20.3 3.2 %gather_fusion.1 = bf16[1024,32]{1,0:T(8,128)(2,1)S(1)} fusion(bf16[32,4096]{0,1:T(8,128)(2,1)S(1)} %copy.32, s32[1024]{0:T(1024)S(1)} %broadcast_clamp_fusion), kind=kCustom, calls=%fused_computation.1 | custom fusion | bytes 135168 | tf_op jit(solution)/shard_map/jit(_take)/gather | solution.py:55
  23.5 0.1 copy.33
  23.6 0.6 select_select_fusion
  24.3 1.1 all-to-all-done.1
  25.4 4.9 %all-to-all-start = ((bf16[32,8,128]{2,0,1:T(8,128)(2,1)}), bf16[32,8,128]{2,0,1:T(8,128)(2,1)S(1)}, u32[]{:S(2)}, u32[]{:S(2)}) async-start(bf16[32,8,128]{2,0,1:T(8,128)(2,1)} %select_select_fusion), calls=%async_computation | async-start | bytes 131072 | tf_op jit(solution)/shard_map/all_to_all | solution.py:64
  30.3 0.0 all-gather.2.cloned.1.call-start
  31.0 0.1 reshape.214
  31.1 0.1 reshape.182
  31.2 5.9 %all-to-all-done = bf16[32,8,128]{2,0,1:T(8,128)(2,1)S(1)} async-done(((bf16[32,8,128]{2,0,1:T(8,128)(2,1)}), bf16[32,8,128]{2,0,1:T(8,128)(2,1)S(1)}, u32[]{:S(2)}, u32[]{:S(2)}) %all-to-all-start) | async-done | bytes 65568 | tf_op jit(solution)/shard_map/all_to_all | solution.py:64
  37.2 1.0 copy_bitcast_fusion
  38.2 0.1 broadcast_in_dim.56
  38.2 0.0 copy-done.3
  38.3 0.0 copy-start.5
  38.3 8.5 %while.11 = (s32[]{:T(128)}, f32[32,32,128]{2,1,0:T(8,128)S(1)}, s32[]{:T(128)}, s32[1,128]{1,0:T(1,128)S(1)}, s32[]{:T(128)}, /*index=5*/bf16[128,128,128]{2,1,...) while((s32[]{:T(128)}, f32[32,32,128]{2,1,0:T(8,128)S(1)}, ...), condition=%wide.region_1.2_spmd.clone, body=%wide.region_0.1_spmd.clone.sunk | while | flops 84151648 | bytes 3937595 | solution.py:96
  38.3 0.1 fusion.44
  38.4 0.1 fusion.43
  38.4 0.7 compare_and_fusion.4
  39.2 0.6 gather_fusion
  39.8 1.9 %convolution_bitcast_fusion.5 = f32[32,32,128]{2,0,1:T(8,128)S(1)} fusion(bf16[128,128,128]{2,1,0:T(8,128)(2,1)} %get-tuple-element.208, s32[]{:T(128)S(6)} %select_n.168, bf16[32,32,128]{2,1,0:T(8,128)(2,1)S(1)} %gather_fusion, pred[32]{0:T(512)(128)(4,1)S(1)} %get-tuple-element.177), kind=kOutput, calls=%fused_computation.5.clone.1 | convolution fusion | flops 33685504 | bytes 1835044 | tf_op jit(solution)/shard_map/while/body/ftk,tik->fti/dot_general | solution.py:84
  41.7 0.8 fusion.45
  42.6 0.1 fusion.44
  42.6 0.1 fusion.43
  42.7 0.7 compare_and_fusion.4
  43.4 0.6 gather_fusion
  44.0 1.9 %convolution_bitcast_fusion.5 = f32[32,32,128]{2,0,1:T(8,128)S(1)} fusion(bf16[128,128,128]{2,1,0:T(8,128)(2,1)} %get-tuple-element.208, s32[]{:T(128)S(6)} %select_n.168, bf16[32,32,128]{2,1,0:T(8,128)(2,1)S(1)} %gather_fusion, pred[32]{0:T(512)(128)(4,1)S(1)} %get-tuple-element.177), kind=kOutput, calls=%fused_computation.5.clone.1 | convolution fusion | flops 33685504 | bytes 1835044 | tf_op jit(solution)/shard_map/while/body/ftk,tik->fti/dot_general | solution.py:84
  46.0 0.8 fusion.45
  46.8 0.0 copy-start.2
  46.9 0.1 convert_element_type.27
  47.0 0.1 collective-permute-start
  47.1 0.0 copy-start.4
  47.1 1.5 collective-permute-done
  48.6 0.1 pad_maximum_fusion.1
  48.7 1.6 collective-permute-start.1
  50.3 0.0 all-gather.2.cloned.1.call-update
  50.3 0.0 all-reduce.2.cloned.1.call-start
  50.4 0.1 dynamic_slice.24
  50.4 12.3 %collective-permute-done.1 = bf16[2,32,4096]{2,1,0:T(8,128)(2,1)S(1)} collective-permute-done((bf16[2,32,4096]{2,1,0:T(8,128)(2,1)S(1)}, bf16[2,32,4096]{2,1,0:T(8,128)(2,1)S(1)}, u32[]{:S(2)}, u32[]{:S(2)}) %collective-permute-start.1) | collective-permute-done | bytes 524320 | tf_op jit(solution)/shard_map/ppermute | solution.py:19
  62.7 0.1 broadcast_select_fusion.1
  62.8 0.1 pad_maximum_fusion
  62.9 9.2 %all-gather.2.cloned.1.call-done = bf16[128,4096]{1,0:T(8,128)(2,1)} async-done(((bf16[32,4096]{1,0:T(8,128)(2,1)}), bf16[128,4096]{1,0:T(8,128)(2,1)}) %all-gather.2.cloned.1.call-update) | async-done | bytes 1048592 | tf_op jit(solution)/shard_map/all_gather | solution.py:103
  72.1 0.0 copy-done.2
  72.1 1.6 %fusion.20 = f32[64,4096]{1,0:T(8,128)S(1)} fusion(bf16[128,4096]{1,0:T(8,128)(2,1)} %all-gather.2.cloned.1.call-done, bf16[128,256]{1,0:T(8,128)(2,1)S(1)} %copy-done.2, s32[]{:T(128)S(6)} %select_n.109), kind=kOutput, calls=%fused_computation.51 | convolution fusion | flops 67108864 | bytes 2129924 | tf_op jit(solution)/shard_map/dot_general | solution.py:108
  73.8 1.7 %convert_reduce_fusion = (f32[64]{0:T(128)S(1)}, bf16[64,4096]{1,0:T(8,128)(2,1)S(1)}, bf16[64,4096]{1,0:T(8,128)(2,1)}) fusion(bf16[64,4096]{1,0:T(8,128)(2,1)S(1)} %copy-done.4, f32[64]{0:T(128)S(1)} %dynamic_slice.24, f32[64,4096]{1,0:T(8,128)S(1)} %fusion.20, bf16[128,4096]{1,0:T(8,128)(2,1)S(1)} %bitcast.86, bf16[128,256]{1,0:T(8,128)(2,1)S(1)} %copy-done, ...), kind=kOutput, calls=%fused_computation.34 | convolution fusion | flops 71303104 | bytes 3703556 | tf_op jit(solution)/shard_map/dot_general | solution.py:111
  75.5 0.5 convolution_bitcast_fusion.2
  76.0 0.0 copy-done.1
  76.0 0.5 convolution_bitcast_fusion.3
  76.5 0.6 pad_maximum_fusion.2
  77.1 0.0 all-reduce.2.cloned.1.call-update
  77.1 24.2 %psum.15 = f32[64]{0:T(128)} all-reduce(f32[64]{0:T(128)S(1)} %get-tuple-element.112), channel_id=1, replica_groups=mesh['nodes'=8,'feat'=4] {'nodes'}, use_global_device_ids=true, to_apply=%region_4.5 | all-reduce | flops 64 | bytes 512 | tf_op jit(solution)/shard_map/psum | solution.py:129
  101.3 48.8 %all-reduce.2.cloned.1.call-done = f32[2,128,64]{1,2,0:T(8,128)} async-done(((f32[2,128,64]{1,2,0:T(8,128)}), f32[2,128,64]{1,2,0:T(8,128)}) %all-reduce.2.cloned.1.call-update) | async-done | bytes 65552 | tf_op jit(solution)/shard_map/psum | solution.py:129
  150.1 1.4 slice_bitcast_fusion
  (14 shorter events, 0.2 us)
Async XLA Ops:
  7.2 66.6 %copy-start = (bf16[128,256]{1,0:T(8,128)(2,1)S(1)}, bf16[128,256]{1,0:T(8,128)(2,1)}, u32[]{:S(2)}) copy-start(bf16[128,256]{1,0:T(8,128)(2,1)} %param.16) | copy-start | bytes 196612
  7.2 31.1 %copy-start.3 = (s32[1,128]{1,0:T(1,128)S(1)}, s32[1,128]{1,0:T(1,128)}, u32[]{:S(2)}) copy-start(s32[1,128]{1,0:T(1,128)} %param.24) | copy-start | bytes 1540
  7.2 31.1 %copy-start.6 = (s32[1,128]{1,0:T(1,128)S(1)}, s32[1,128]{1,0:T(1,128)}, u32[]{:S(2)}) copy-start(s32[1,128]{1,0:T(1,128)} %param.23) | copy-start | bytes 1540
  11.5 13.9 %all-to-all-start.1 = ((bf16[8,2,512]{2,1,0:T(2,128)(2,1)}), bf16[8,2,512]{2,1,0:T(2,128)(2,1)S(1)}, u32[]{:S(2)}, u32[]{:S(2)}) async-start(bf16[8,2,512]{2,1,0:T(2,128)(2,1)} %reshape.213), calls=%async_computation.1 | async-start | bytes 32768 | tf_op jit(solution)/shard_map/all_to_all | solution.py:65
  25.4 11.8 %all-to-all-start = ((bf16[32,8,128]{2,0,1:T(8,128)(2,1)}), bf16[32,8,128]{2,0,1:T(8,128)(2,1)S(1)}, u32[]{:S(2)}, u32[]{:S(2)}) async-start(bf16[32,8,128]{2,0,1:T(8,128)(2,1)} %select_select_fusion), calls=%async_computation | async-start | bytes 131072 | tf_op jit(solution)/shard_map/all_to_all | solution.py:64
  30.3 41.8 %all-gather.2.cloned.1.call-start = ((), (), s32[]{:S(2)}) async-start(), calls=%async_computation.2 | async-start | bytes 1310720 | tf_op jit(solution)/shard_map/all_gather | solution.py:103
  38.3 12.1 %copy-start.5 = (f32[256]{0:T(256)S(1)}, f32[256]{0:T(256)}, u32[]{:S(2)}) copy-start(f32[256]{0:T(256)} %param.17) | copy-start | bytes 3076
  46.8 25.3 %copy-start.2 = (bf16[128,256]{1,0:T(8,128)(2,1)S(1)}, bf16[128,256]{1,0:T(8,128)(2,1)}, u32[]{:S(2)}) copy-start(bf16[128,256]{1,0:T(8,128)(2,1)} %param.15) | copy-start | bytes 196612
  47.0 1.6 %collective-permute-start = (bf16[1,32,4096]{2,1,0:T(8,128)(2,1)S(1)}, bf16[1,32,4096]{2,1,0:T(8,128)(2,1)S(1)}, u32[]{:S(2)}, u32[]{:S(2)}) collective-permute-start(bf16[1,32,4096]{2,1,0:T(8,128)(2,1)S(1)} %convert_element_type.27), channel_id=1, source_target_pairs={{0,1},{1,0},{2,3},{3,2},{4,5},{5,4},{6,7},{7,6},{8,9},{9,8},{10,11... | collective-permute-start | bytes 786440 | tf_op jit(solution)/shard_map/ppermute | solution.py:19
  47.1 26.7 %copy-start.4 = (bf16[64,4096]{1,0:T(8,128)(2,1)S(1)}, bf16[64,4096]{1,0:T(8,128)(2,1)}, u32[]{:S(2)}) copy-start(bf16[64,4096]{1,0:T(8,128)(2,1)} %param.18) | copy-start | bytes 1572868
  48.7 14.0 %collective-permute-start.1 = (bf16[2,32,4096]{2,1,0:T(8,128)(2,1)S(1)}, bf16[2,32,4096]{2,1,0:T(8,128)(2,1)S(1)}, u32[]{:S(2)}, u32[]{:S(2)}) collective-permute-start(bf16[2,32,4096]{2,1,0:T(8,128)(2,1)S(1)} %pad_maximum_fusion.1), channel_id=1, source_target_pairs={{0,2},{1,3},{2,0},{3,1},{4,6},{5,7},{6,4},{7,5},{8,10},{9,11},{10,... | collective-permute-start | bytes 1572872 | tf_op jit(solution)/shard_map/ppermute | solution.py:19
  50.3 99.8 %all-reduce.2.cloned.1.call-start = ((), (), s32[]{:S(2)}) async-start(), calls=%async_computation.3 | async-start | bytes 131072 | tf_op jit(solution)/shard_map/psum | solution.py:129
  73.8 2.2 %copy-start.1 = (bf16[128,4096]{1,0:T(8,128)(2,1)S(1)}, bf16[128,4096]{1,0:T(8,128)(2,1)}, u32[]{:S(2)}) copy-start(bf16[128,4096]{1,0:T(8,128)(2,1)} %all-gather.2.cloned.1.call-done) | copy-start | bytes 3145732
Sparse Core Ops, SparseCore 0:
  50.4 21.6 all-gather.1
  77.2 72.7 all-reduce.1
